TPU v7x, 512 devices: a whole 4x4x16 slice. The times are simulated.
512 devices in a mesh: box: 128 (over z, y, core), level: 4 (over x).
Axes of the slice: x: 4, y: 4, z: 16, core: 2. Of those that a mesh axis runs over, the one named last changes fastest.
Arguments:
- rhs_field: float32 [4, 2048, 128], P(None, 'box'), may hold values from -6 to 6
- self_coef: float32 [2048, 128], P('box'), may hold values from 2 to 4
- expand: bfloat16 [2048, 256, 128], P('box'), may hold values from -0.5 to 0.5
- near_ops: bfloat16 [26, 128, 128], replicated, may hold values from -0.109375 to 0.109375
- class_ops: bfloat16 [128, 256, 256], P('box', 'level'), may hold values from -0.046875 to 0.046875
- near_src: int32 [2048, 26], P('box'), may hold values from 0 to 47
- send_rows: int32 [128, 128, 2], P('box'), may hold values from 0 to 15
- list_slot: int32 [2048, 64], P('box'), may hold values from 0 to 255
- list_class: int32 [2048, 64], P('box'), may hold values from 0 to 127, all different within a row
Outputs:
- solution: float32 [4, 2048, 128], P(None, 'box')
Inputs may be any that keep to these rules, and one draw needn't show every extreme that they name: `near_src`: the near-field neighbours of a box lie among the boxes of the index of box before it, its own and the one after it, counted in that order. `send_rows`: each entry is a box of the sending index. `list_slot`: entry q * 2 + j names the j-th row sent by index q of box. `list_class`: the classes of one box's list are distinct.
All inputs are finite; a program needn't handle non-finite values.
Results may differ from a plain program's by a relative error of at most 0.004.
Values may be sent and summed in bfloat16 or wider, within the bound.
A program may use at most 64 MiB of HBM per device.

v0:
```python
import math
import jax
import jax.numpy as jnp
from jax import lax
from jax.sharding import PartitionSpec as P


def extended_2(block, sides, width):
    for axis, dim in sides:
        count = lax.axis_size(axis)
        forward = [(i, i + 1) for i in range(count - 1)]
        backward = [(target, source) for source, target in forward]
        low = lax.ppermute(
            lax.slice_in_dim(block, block.shape[dim] - width, None, axis=dim), axis, forward
        )
        high = lax.ppermute(lax.slice_in_dim(block, 0, width, axis=dim), axis, backward)
        block = jnp.concatenate([low, block, high], axis=dim)
    return block


def slot_table(list_slot, list_class, classes):
    labels = jnp.arange(classes, dtype=jnp.int32)
    matches = list_class[:, :, None] == labels[None, None, :]
    return jnp.sum(jnp.where(matches, list_slot[:, :, None] + 1, 0), axis=1) - 1


def apply_classes(totals, operators, offset, table, received):
    count = operators.shape[0]
    picked = lax.dynamic_slice_in_dim(table, offset, count, 1)
    sources = jnp.where(
        (picked >= 0)[:, :, None, None],
        received[jnp.maximum(picked, 0)],
        jnp.zeros((), received.dtype),
    )
    return totals + jnp.einsum(
        "cqp,tcrp->trq", operators, sources, preferred_element_type=jnp.float32
    )


def fold_classes(totals, pieces, offset, table, received):
    count = pieces.shape[0]
    stride = math.gcd(count, 16)

    def step_once(number, current):
        operators = lax.dynamic_slice_in_dim(pieces, number * stride, stride, 0)
        return apply_classes(current, operators, offset + number * stride, table, received)

    return lax.fori_loop(0, count // stride, step_once, totals)


def inner(first, second):
    return jnp.sum(first * second, axis=(1, 2))


def spread(values, field):
    return values[:, None, None] * field


def per_device(
    rhs_field, self_coef, expand, near_ops, class_ops, near_src, send_rows, list_slot, list_class
):
    boxes = expand.shape[0]
    band = class_ops.shape[1]
    classes = class_ops.shape[0] * lax.axis_size("box")
    table = slot_table(list_slot, list_class, classes)
    level_index = lax.axis_index("level")
    cached = lax.all_gather(class_ops, "box", axis=0, tiled=True)

    def apply_matrix(field):
        field_half = field.astype(jnp.bfloat16)
        multipoles = jnp.einsum(
            "tpk,rtk->trp", expand, field_half, preferred_element_type=jnp.float32
        ).astype(jnp.bfloat16)
        outgoing = multipoles[send_rows[0]]
        received = lax.all_to_all(outgoing, "box", split_axis=0, concat_axis=0, tiled=True)
        received = received.reshape((-1,) + received.shape[2:])
        extended = extended_2(field_half, (("box", 1),), boxes)
        neighbours = extended[:, near_src]
        near_part = jnp.einsum(
            "kij,rtkj->rti", near_ops, neighbours, preferred_element_type=jnp.float32
        )
        empty = jnp.zeros((boxes, field.shape[0], band), jnp.float32)
        local_full = fold_classes(empty, cached, 0, table, received)
        local_half = local_full.astype(jnp.bfloat16)
        expand_rows = lax.dynamic_slice_in_dim(expand, level_index * band, band, 1)
        partial_field = jnp.einsum(
            "tqk,trq->rtk", expand_rows, local_half, preferred_element_type=jnp.float32
        )
        far_part = lax.psum(partial_field.astype(jnp.bfloat16), "level").astype(jnp.float32)
        return self_coef[None] * field + near_part + far_part

    def totals(*pairs):
        stacked = jnp.stack([inner(a, b) for a, b in pairs])
        return jnp.sum(lax.all_gather(stacked, "box"), axis=0)

    first_image = apply_matrix(rhs_field)
    rr, ra = totals((rhs_field, rhs_field), (rhs_field, first_image))
    h_one_one = ra / rr
    second = first_image - spread(h_one_one, rhs_field)
    second_image = apply_matrix(second)
    uu, rb, ub, bb = totals(
        (second, second),
        (rhs_field, second_image),
        (second, second_image),
        (second_image, second_image),
    )
    beta = jnp.sqrt(rr)
    length = jnp.sqrt(uu)
    h_two_one = length / beta
    h_one_two = rb / (beta * length)
    h_two_two = ub / uu
    gram_aa = h_one_one * h_one_one + h_two_one * h_two_one
    gram_ab = h_one_one * h_one_two + h_two_one * h_two_two
    gram_bb = bb / uu
    right_a = beta * h_one_one
    right_b = beta * h_one_two
    determinant = gram_aa * gram_bb - gram_ab * gram_ab
    coef_a = (gram_bb * right_a - gram_ab * right_b) / determinant
    coef_b = (gram_aa * right_b - gram_ab * right_a) / determinant
    return spread(coef_a / beta, rhs_field) + spread(coef_b / length, second)


def solution(mesh):
    return jax.shard_map(
        per_device,
        mesh=mesh,
        in_specs=(
            P(None, "box", None),
            P("box", None),
            P("box", None, None),
            P(),
            P("box", "level", None),
            P("box", None),
            P("box", None, None),
            P("box", None),
            P("box", None),
        ),
        out_specs=P(None, "box", None),
        check_vma=False,
    )
```

profile of v0, /device:TPU:1, one launch (start us, length us, event | category | flops | bytes accessed | tf_op | source)
XLA Modules:
  0.0 477.1 jit_solution(12812204908708037069)
XLA Ops:
  9.4 1.9 gather_fusion.3
  11.3 20.6 %all-to-all-start = ((bf16[128,2,4,256]{3,2,1,0:T(4,128)(2,1)}), bf16[128,2,4,256]{3,2,1,0:T(4,128)(2,1)S(1)}, u32[]{:S(2)}, u32[]{:S(2)}) async-start(bf16[128,2,4,256]{3,2,1,0:T(4,128)(2,1)} %bitcast.6), calls=%async_computation | async-start | bytes 1048576 | tf_op jit(solution)/shard_map/all_to_all | solution.py:75
  31.9 2.8 collective-permute-start.1
  34.7 2.8 collective-permute-start
  40.1 2.2 gather_fusion.2
  42.3 21.9 %all-to-all-done = bf16[128,2,4,256]{3,2,1,0:T(4,128)(2,1)S(1)} async-done(((bf16[128,2,4,256]{3,2,1,0:T(4,128)(2,1)}), bf16[128,2,4,256]{3,2,1,0:T(4,128)(2,1)S(1)}, u32[]{:S(2)}, u32[]{:S(2)}) %all-to-all-start) | async-done | bytes 524320 | tf_op jit(solution)/shard_map/all_to_all | solution.py:75
  64.2 96.6 %all-gather.6.cloned.1.call-done = bf16[128,64,256]{2,1,0:T(8,128)(2,1)} async-done(((bf16[1,64,256]{2,1,0:T(8,128)(2,1)}), bf16[128,64,256]{2,1,0:T(8,128)(2,1)}) %all-gather.6.cloned.1.call-update) | async-done | bytes 4194320 | tf_op jit(solution)/shard_map/all_gather | solution.py:67
  160.8 24.6 %while.28 = (s32[]{:T(128)}, f32[16,4,64]{2,0,1:T(8,128)S(1)}, s32[16,128]{1,0:T(8,128)S(1)}, bf16[256,4,256]{2,1,0:T(4,128)(2,1)S(1)}, bf16[128,64,256]{2,1,0:T...) while((s32[]{:T(128)}, f32[16,4,64]{2,0,1:T(8,128)S(1)}, ...), condition=%wide.region_2.3_spmd.clone, body=%wide.region_1.2_spmd.clone.sunk | while | flops 33826312 | bytes 2142377 | solution.py:48
  165.4 1.5 fusion.51
  168.5 1.5 fusion.51
  171.5 1.5 fusion.51
  180.8 1.5 fusion.51
  183.8 1.5 fusion.51
  185.6 13.1 %psum.14 = bf16[4,16,128]{2,1,0:T(8,128)(2,1)S(1)} all-reduce(bf16[4,16,128]{2,1,0:T(8,128)(2,1)S(1)} %bitcast.147), channel_id=1, replica_groups=mesh['box'=128,'level'=4] {'level'}, use_global_device_ids=true, to_apply=%region_3.4 | all-reduce | flops 8192 | bytes 32768 | tf_op jit(solution)/shard_map/psum | solution.py:89
  199.2 84.8 %all-gather.2 = f32[128,2,4]{2,1,0:T(2,128)S(1)} all-gather(f32[1,2,4]{2,1,0:T(2,128)S(1)} %maximum_bitcast_fusion.1), channel_id=2, replica_groups=mesh['box'=128,'level'=4] {'box'}, dimensions={0}, use_global_device_ids=true | all-gather | bytes 4128 | tf_op jit(solution)/shard_map/all_gather | solution.py:94
  284.7 1.9 gather_fusion.5
  286.6 10.3 %all-to-all-start.1 = ((bf16[128,2,4,256]{3,2,1,0:T(4,128)(2,1)}), bf16[128,2,4,256]{3,2,1,0:T(4,128)(2,1)S(1)}, u32[]{:S(2)}, u32[]{:S(2)}) async-start(bf16[128,2,4,256]{3,2,1,0:T(4,128)(2,1)} %bitcast.18), calls=%async_computation.1 | async-start | bytes 1048576 | tf_op jit(solution)/shard_map/all_to_all | solution.py:75
  296.9 2.8 collective-permute-start.3
  299.7 2.9 collective-permute-start.2
  303.4 2.2 gather_fusion.4
  305.6 22.2 %all-to-all-done.1 = bf16[128,2,4,256]{3,2,1,0:T(4,128)(2,1)S(1)} async-done(((bf16[128,2,4,256]{3,2,1,0:T(4,128)(2,1)}), bf16[128,2,4,256]{3,2,1,0:T(4,128)(2,1)S(1)}, u32[]{:S(2)}, u32[]{:S(2)}) %all-to-all-start.1) | async-done | bytes 524320 | tf_op jit(solution)/shard_map/all_to_all | solution.py:75
  327.7 24.5 %while.29 = (s32[]{:T(128)}, f32[16,4,64]{2,0,1:T(8,128)S(1)}, s32[16,128]{1,0:T(8,128)S(1)}, bf16[256,4,256]{2,1,0:T(4,128)(2,1)S(1)}, bf16[128,64,256]{2,1,0:T...) while((s32[]{:T(128)}, f32[16,4,64]{2,0,1:T(8,128)S(1)}, ...), condition=%wide.region_9.10_spmd.clone, body=%wide.region_8.9_spmd.clone.sunk | while | flops 33826312 | bytes 2142377 | solution.py:48
  352.4 10.8 %psum.15 = bf16[4,16,128]{2,1,0:T(8,128)(2,1)S(1)} all-reduce(bf16[4,16,128]{2,1,0:T(8,128)(2,1)S(1)} %bitcast.148), channel_id=1, replica_groups=mesh['box'=128,'level'=4] {'level'}, use_global_device_ids=true, to_apply=%region_10.11 | all-reduce | flops 8192 | bytes 32768 | tf_op jit(solution)/shard_map/psum | solution.py:89
  363.8 105.6 %all-gather.3 = f32[128,4,4]{2,1,0:T(4,128)S(1)} all-gather(f32[1,4,4]{2,1,0:T(4,128)S(1)} %maximum_bitcast_fusion), channel_id=3, replica_groups=mesh['box'=128,'level'=4] {'box'}, dimensions={0}, use_global_device_ids=true | all-gather | bytes 8256 | tf_op jit(solution)/shard_map/all_gather | solution.py:94
  (156 shorter events, 49.8 us)
Async XLA Ops:
  6.5 2.5 copy-start
  6.5 154.3 %all-gather.6.cloned.1.call-start = ((), (), s32[]{:S(2)}) async-start(), calls=%async_computation.2 | async-start | bytes 4227072 | tf_op jit(solution)/shard_map/all_gather | solution.py:67
  11.3 52.9 %all-to-all-start = ((bf16[128,2,4,256]{3,2,1,0:T(4,128)(2,1)}), bf16[128,2,4,256]{3,2,1,0:T(4,128)(2,1)S(1)}, u32[]{:S(2)}, u32[]{:S(2)}) async-start(bf16[128,2,4,256]{3,2,1,0:T(4,128)(2,1)} %bitcast.6), calls=%async_computation | async-start | bytes 1048576 | tf_op jit(solution)/shard_map/all_to_all | solution.py:75
  31.9 8.2 %collective-permute-start.1 = (bf16[4,16,128]{2,0,1:T(4,128)(2,1)S(1)}, bf16[4,16,128]{2,0,1:T(4,128)(2,1)S(1)}, u32[]{:S(2)}, u32[]{:S(2)}) collective-permute-start(bf16[4,16,128]{2,0,1:T(4,128)(2,1)S(1)} %copy.87), channel_id=1, source_target_pairs={{4,0},{8,4},{12,8},{16,12},{20,16},{24,20},{28,24},{32,28},{36,32}... | collective-permute-start | bytes 49160 | tf_op jit(solution)/shard_map/ppermute | solution.py:16
  34.7 5.4 %collective-permute-start = (bf16[4,16,128]{2,0,1:T(4,128)(2,1)S(1)}, bf16[4,16,128]{2,0,1:T(4,128)(2,1)S(1)}, u32[]{:S(2)}, u32[]{:S(2)}) collective-permute-start(bf16[4,16,128]{2,0,1:T(4,128)(2,1)S(1)} %copy.87), channel_id=1, source_target_pairs={{0,4},{4,8},{8,12},{12,16},{16,20},{20,24},{24,28},{28,32},{32,36}... | collective-permute-start | bytes 49160 | tf_op jit(solution)/shard_map/ppermute | solution.py:13
  160.8 37.9 %copy-start.1 = (bf16[26,128,128]{2,1,0:T(8,128)(2,1)S(1)}, bf16[26,128,128]{2,1,0:T(8,128)(2,1)}, u32[]{:S(2)}) copy-start(bf16[26,128,128]{2,1,0:T(8,128)(2,1)} %param.16) | copy-start | bytes 2555908
  160.8 37.9 %copy-start.2 = (f32[4,16,128]{2,1,0:T(8,128)S(1)}, f32[4,16,128]{2,1,0:T(8,128)}, u32[]{:S(2)}) copy-start(f32[4,16,128]{2,1,0:T(8,128)} %param.13) | copy-start | bytes 98308
  160.8 37.9 %copy-start.3 = (f32[16,128]{1,0:T(8,128)S(1)}, f32[16,128]{1,0:T(8,128)}, u32[]{:S(2)}) copy-start(f32[16,128]{1,0:T(8,128)} %param.14) | copy-start | bytes 24580
  286.6 41.2 %all-to-all-start.1 = ((bf16[128,2,4,256]{3,2,1,0:T(4,128)(2,1)}), bf16[128,2,4,256]{3,2,1,0:T(4,128)(2,1)S(1)}, u32[]{:S(2)}, u32[]{:S(2)}) async-start(bf16[128,2,4,256]{3,2,1,0:T(4,128)(2,1)} %bitcast.18), calls=%async_computation.1 | async-start | bytes 1048576 | tf_op jit(solution)/shard_map/all_to_all | solution.py:75
  296.9 5.8 %collective-permute-start.3 = (bf16[4,16,128]{2,1,0:T(8,128)(2,1)S(1)}, bf16[4,16,128]{2,1,0:T(8,128)(2,1)S(1)}, u32[]{:S(2)}, u32[]{:S(2)}) collective-permute-start(bf16[4,16,128]{2,1,0:T(8,128)(2,1)S(1)} %get-tuple-element.261), channel_id=1, source_target_pairs={{4,0},{8,4},{12,8},{16,12},{20,16},{24,20},{28,24},{32,28},{36,32}... | collective-permute-start | bytes 49160 | tf_op jit(solution)/shard_map/ppermute | solution.py:16
  299.7 3.6 collective-permute-start.2
Sparse Core Ops, SparseCore 0:
  10.5 150.2 all-gather.5
where the time goes:
time: 478 us; the launch traced here: 477 us
  blocking collectives  214 us (45%)
  waiting for transfers between devices  142 us (30%)
  starting transfers between devices  42.2 us (9%)
  local copies, waits for them, and re-layouts  30.7 us (6%)
  matrix products  26.8 us (6%)
  between operations  13.6 us (3%)
  other arithmetic  6.97 us (1%)
    all_gather x2, blocking collectives, totals(): return jnp.sum(lax.all_gather(stacked, 'box'), axis=0)  190 us
    all_gather x1, waiting for transfers between devices, per_device(): cached = lax.all_gather(class_ops, 'box', axis=0, tiled=True)  96.6 us
    all_to_all x2, waiting for transfers between devices, apply_matrix(): lax.all_to_all(outgoing, 'box', split_axis=0, concat_axis=0, tiled=True)  44.1 us
    all_to_all x2, starting transfers between devices, apply_matrix(): lax.all_to_all(outgoing, 'box', split_axis=0, concat_axis=0, tiled=True)  30.9 us
    dot_general x16, matrix products, apply_classes(): jnp.einsum('cqp,tcrp->trq', operators, sources, preferred_element_type=jn...  24.6 us
    psum x2, blocking collectives, apply_matrix(): lax.psum(partial_field.astype(jnp.bfloat16), 'level').astype(jnp.float32)  23.9 us
    gather x16, local copies, waits for them, and re-layouts, apply_classes(): received[jnp.maximum(picked, 0)]  18.5 us
  transfers between devices with their start and end apart: 7, of which 4 were waited for; matrix products, arithmetic and copies ran while one was open for 2% of the time, Pallas kernels for 0%

commit v1 on v0

--- a/solution.py
+++ b/solution.py
@@ -64,7 +64,9 @@
     classes = class_ops.shape[0] * lax.axis_size("box")
     table = slot_table(list_slot, list_class, classes)
     level_index = lax.axis_index("level")
-    cached = lax.all_gather(class_ops, "box", axis=0, tiled=True)
+    cached = jnp.concatenate(
+        lax.all_to_all(jnp.stack([class_ops] * lax.axis_size("box")), "box", 0, 0), axis=0
+    )
 
     def apply_matrix(field):
         field_half = field.astype(jnp.bfloat16)

time: 478 us -> 567 us (1.19)
  blocking collectives: 214 us -> 271 us
  waiting for transfers between devices: 142 us -> 198 us
  between operations: 13.6 us -> 0.28 us
  starting transfers between devices: 42.2 us -> 30.8 us
    all_to_all x0 -> x1, waiting for transfers between devices: none -> 172 us  [per_device(): lax.all_to_all(jnp.stack([class_ops] * lax.axis_size('box')), 'box', 0, 0)]
    all_gather x1 -> x0, waiting for transfers between devices: 96.6 us -> none  [per_device(): cached = lax.all_gather(class_ops, 'box', axis=0, tiled=True)]
    all_to_all x0 -> x1, blocking collectives: none -> 51.2 us  [apply_matrix(): lax.all_to_all(outgoing, 'box', split_axis=0, concat_axis=0, tiled=True)]
    all_to_all x2 -> x1, waiting for transfers between devices: 44.1 us -> 19.7 us  [apply_matrix(): lax.all_to_all(outgoing, 'box', split_axis=0, concat_axis=0, tiled=True)]
    all_to_all x2 -> x1, starting transfers between devices: 30.9 us -> 10.2 us  [apply_matrix(): lax.all_to_all(outgoing, 'box', split_axis=0, concat_axis=0, tiled=True)]
    all_to_all x0 -> x1, starting transfers between devices: none -> 9.7 us  [per_device(): lax.all_to_all(jnp.stack([class_ops] * lax.axis_size('box')), 'box', 0, 0)]
    ppermute x2, waiting for transfers between devices: 0.01 us -> 6.56 us  [extended_2(): lax.ppermute(lax.slice_in_dim(block, 0, width, axis=dim), axis, backward)]
    all_gather x2, blocking collectives: 190 us -> 196 us  [totals(): return jnp.sum(lax.all_gather(stacked, 'box'), axis=0)]
  transfers between devices with their start and end apart: 7 -> 6, of which waited for: 4 -> 4; matrix products, arithmetic and copies ran while one was open for 2% -> 1% of each run, Pallas kernels for 0% -> 0%
where the time goes in v1:
time: 567 us; the launch traced here: 566 us
  blocking collectives  271 us (48%)
  waiting for transfers between devices  198 us (35%)
  local copies, waits for them, and re-layouts  33.2 us (6%)
  starting transfers between devices  30.8 us (5%)
  matrix products  26.7 us (5%)
    all_gather x2, blocking collectives, totals(): return jnp.sum(lax.all_gather(stacked, 'box'), axis=0)  196 us
    all_to_all x1, waiting for transfers between devices, per_device(): lax.all_to_all(jnp.stack([class_ops] * lax.axis_size('box')), 'box', 0, 0)  172 us
    all_to_all x1, blocking collectives, apply_matrix(): lax.all_to_all(outgoing, 'box', split_axis=0, concat_axis=0, tiled=True)  51.2 us
    dot_general x16, matrix products, apply_classes(): jnp.einsum('cqp,tcrp->trq', operators, sources, preferred_element_type=jn...  24.5 us
    psum x2, blocking collectives, apply_matrix(): lax.psum(partial_field.astype(jnp.bfloat16), 'level').astype(jnp.float32)  24 us
    all_to_all x1, waiting for transfers between devices, apply_matrix(): lax.all_to_all(outgoing, 'box', split_axis=0, concat_axis=0, tiled=True)  19.7 us
    gather x16, local copies, waits for them, and re-layouts, apply_classes(): received[jnp.maximum(picked, 0)]  18.5 us
  transfers between devices with their start and end apart: 6, of which 4 were waited for; matrix products, arithmetic and copies ran while one was open for 1% of the time, Pallas kernels for 0%

profile of v1, /device:TPU:1, one launch (start us, length us, event | category | flops | bytes accessed | tf_op | source)
XLA Modules:
  0.0 566.0 jit_solution(11493455042842846594)
XLA Ops:
  3.4 51.2 %all_to_all.15 = bf16[128,2,4,256]{3,2,1,0:T(4,128)(2,1)S(1)} all-to-all(bf16[128,2,4,256]{3,2,1,0:T(4,128)(2,1)S(1)} %bitcast.149), channel_id=1, replica_groups=mesh['box'=128,'level'=4] {'box'}, dimensions={0} | all-to-all | bytes 1048576 | tf_op jit(solution)/shard_map/all_to_all | solution.py:77
  54.6 3.2 stack.18
  57.8 9.7 %all-to-all-start.1 = ((bf16[128,1,64,256]{3,2,1,0:T(8,128)(2,1)}), bf16[128,1,64,256]{3,2,1,0:T(8,128)(2,1)}, u32[]{:S(2)}, u32[]{:S(2)}) async-start(bf16[128,1,64,256]{3,2,1,0:T(8,128)(2,1)} %stack.18), calls=%async_computation.1 | async-start | bytes 8388608 | tf_op jit(solution)/shard_map/all_to_all | solution.py:68
  67.5 3.5 collective-permute-start
  71.1 1.9 collective-permute-start.1
  73.5 3.1 collective-permute-done.1
  76.7 2.2 gather_fusion.2
  78.9 172.1 %all-to-all-done.1 = bf16[128,1,64,256]{3,2,1,0:T(8,128)(2,1)} async-done(((bf16[128,1,64,256]{3,2,1,0:T(8,128)(2,1)}), bf16[128,1,64,256]{3,2,1,0:T(8,128)(2,1)}, u32[]{:S(2)}, u32[]{:S(2)}) %all-to-all-start.1) | async-done | bytes 4194336 | tf_op jit(solution)/shard_map/all_to_all | solution.py:68
  251.0 24.4 %while.28 = (s32[]{:T(128)}, f32[16,4,64]{2,0,1:T(8,128)S(1)}, s32[16,128]{1,0:T(8,128)S(1)}, bf16[256,4,256]{2,1,0:T(4,128)(2,1)S(1)}, bf16[128,64,256]{2,1,0:T...) while((s32[]{:T(128)}, f32[16,4,64]{2,0,1:T(8,128)S(1)}, ...), condition=%wide.region_2.3_spmd.clone, body=%wide.region_1.2_spmd.clone.sunk | while | flops 33826312 | bytes 2142369 | solution.py:48
  273.9 1.5 fusion.51
  275.7 13.1 %psum.14 = bf16[4,16,128]{2,1,0:T(8,128)(2,1)S(1)} all-reduce(bf16[4,16,128]{2,1,0:T(8,128)(2,1)S(1)} %bitcast.150), channel_id=1, replica_groups=mesh['box'=128,'level'=4] {'level'}, use_global_device_ids=true, to_apply=%region_3.4 | all-reduce | flops 8192 | bytes 32768 | tf_op jit(solution)/shard_map/psum | solution.py:91
  289.4 90.5 %all-gather.2 = f32[128,2,4]{2,1,0:T(2,128)S(1)} all-gather(f32[1,2,4]{2,1,0:T(2,128)S(1)} %maximum_bitcast_fusion.1), channel_id=2, replica_groups=mesh['box'=128,'level'=4] {'box'}, dimensions={0}, use_global_device_ids=true | all-gather | bytes 4128 | tf_op jit(solution)/shard_map/all_gather | solution.py:96
  380.5 1.9 gather_fusion.5
  382.4 10.2 %all-to-all-start.2 = ((bf16[128,2,4,256]{3,2,1,0:T(4,128)(2,1)}), bf16[128,2,4,256]{3,2,1,0:T(4,128)(2,1)S(1)}, u32[]{:S(2)}, u32[]{:S(2)}) async-start(bf16[128,2,4,256]{3,2,1,0:T(4,128)(2,1)} %bitcast.20), calls=%async_computation.2 | async-start | bytes 1048576 | tf_op jit(solution)/shard_map/all_to_all | solution.py:77
  392.7 3.5 collective-permute-start.2
  396.2 1.9 collective-permute-start.3
  398.2 3.4 collective-permute-done.3
  401.6 2.2 gather_fusion.4
  403.8 19.7 %all-to-all-done.2 = bf16[128,2,4,256]{3,2,1,0:T(4,128)(2,1)S(1)} async-done(((bf16[128,2,4,256]{3,2,1,0:T(4,128)(2,1)}), bf16[128,2,4,256]{3,2,1,0:T(4,128)(2,1)S(1)}, u32[]{:S(2)}, u32[]{:S(2)}) %all-to-all-start.2) | async-done | bytes 524320 | tf_op jit(solution)/shard_map/all_to_all | solution.py:77
  423.5 24.4 %while.29 = (s32[]{:T(128)}, f32[16,4,64]{2,0,1:T(8,128)S(1)}, s32[16,128]{1,0:T(8,128)S(1)}, bf16[256,4,256]{2,1,0:T(4,128)(2,1)S(1)}, bf16[128,64,256]{2,1,0:T...) while((s32[]{:T(128)}, f32[16,4,64]{2,0,1:T(8,128)S(1)}, ...), condition=%wide.region_9.10_spmd.clone, body=%wide.region_8.9_spmd.clone.sunk | while | flops 33826312 | bytes 2142369 | solution.py:48
  425.0 1.5 fusion.53
  428.0 1.5 fusion.53
  448.1 10.8 %psum.15 = bf16[4,16,128]{2,1,0:T(8,128)(2,1)S(1)} all-reduce(bf16[4,16,128]{2,1,0:T(8,128)(2,1)S(1)} %bitcast.151), channel_id=1, replica_groups=mesh['box'=128,'level'=4] {'level'}, use_global_device_ids=true, to_apply=%region_10.11 | all-reduce | flops 8192 | bytes 32768 | tf_op jit(solution)/shard_map/psum | solution.py:91
  459.5 105.6 %all-gather.3 = f32[128,4,4]{2,1,0:T(4,128)S(1)} all-gather(f32[1,4,4]{2,1,0:T(4,128)S(1)} %maximum_bitcast_fusion), channel_id=3, replica_groups=mesh['box'=128,'level'=4] {'box'}, dimensions={0}, use_global_device_ids=true | all-gather | bytes 8256 | tf_op jit(solution)/shard_map/all_gather | solution.py:96
  (161 shorter events, 50.6 us)
Async XLA Ops:
  0.0 1.8 copy-start
  57.8 15.2 %copy-start.5 = (s32[16,26]{1,0:T(8,128)S(1)}, s32[16,26]{1,0:T(8,128)}, u32[]{:S(2)}) copy-start(s32[16,26]{1,0:T(8,128)} %param.18) | copy-start | bytes 4996
  57.8 15.3 %copy-start.6 = (s32[16,64]{1,0:T(8,128)S(1)}, s32[16,64]{1,0:T(8,128)}, u32[]{:S(2)}) copy-start(s32[16,64]{1,0:T(8,128)} %param.20) | copy-start | bytes 12292
  57.8 15.3 %copy-start.4 = (s32[16,64]{1,0:T(8,128)S(1)}, s32[16,64]{1,0:T(8,128)}, u32[]{:S(2)}) copy-start(s32[16,64]{1,0:T(8,128)} %param.21) | copy-start | bytes 12292
  57.8 193.2 %all-to-all-start.1 = ((bf16[128,1,64,256]{3,2,1,0:T(8,128)(2,1)}), bf16[128,1,64,256]{3,2,1,0:T(8,128)(2,1)}, u32[]{:S(2)}, u32[]{:S(2)}) async-start(bf16[128,1,64,256]{3,2,1,0:T(8,128)(2,1)} %stack.18), calls=%async_computation.1 | async-start | bytes 8388608 | tf_op jit(solution)/shard_map/all_to_all | solution.py:68
  67.5 6.0 %collective-permute-start = (bf16[4,16,128]{2,0,1:T(4,128)(2,1)S(1)}, bf16[4,16,128]{2,0,1:T(4,128)(2,1)S(1)}, u32[]{:S(2)}, u32[]{:S(2)}) collective-permute-start(bf16[4,16,128]{2,0,1:T(4,128)(2,1)S(1)} %copy.87), channel_id=1, source_target_pairs={{0,4},{4,8},{8,12},{12,16},{16,20},{20,24},{24,28},{28,32},{32,36}... | collective-permute-start | bytes 49160 | tf_op jit(solution)/shard_map/ppermute | solution.py:13
  71.1 5.6 collective-permute-start.1
  251.0 37.8 %copy-start.1 = (bf16[26,128,128]{2,1,0:T(8,128)(2,1)S(1)}, bf16[26,128,128]{2,1,0:T(8,128)(2,1)}, u32[]{:S(2)}) copy-start(bf16[26,128,128]{2,1,0:T(8,128)(2,1)} %param.16) | copy-start | bytes 2555908
  251.0 37.8 %copy-start.2 = (f32[4,16,128]{2,1,0:T(8,128)S(1)}, f32[4,16,128]{2,1,0:T(8,128)}, u32[]{:S(2)}) copy-start(f32[4,16,128]{2,1,0:T(8,128)} %param.13) | copy-start | bytes 98308
  251.0 37.8 %copy-start.3 = (f32[16,128]{1,0:T(8,128)S(1)}, f32[16,128]{1,0:T(8,128)}, u32[]{:S(2)}) copy-start(f32[16,128]{1,0:T(8,128)} %param.14) | copy-start | bytes 24580
  382.4 41.1 %all-to-all-start.2 = ((bf16[128,2,4,256]{3,2,1,0:T(4,128)(2,1)}), bf16[128,2,4,256]{3,2,1,0:T(4,128)(2,1)S(1)}, u32[]{:S(2)}, u32[]{:S(2)}) async-start(bf16[128,2,4,256]{3,2,1,0:T(4,128)(2,1)} %bitcast.20), calls=%async_computation.2 | async-start | bytes 1048576 | tf_op jit(solution)/shard_map/all_to_all | solution.py:77
  392.7 5.5 collective-permute-start.2
  396.2 5.4 collective-permute-start.3
